TPU v7x, 32 devices: a whole 2x2x4 slice. The times are simulated.
32 devices in a mesh: freq: 2 (over x), row: 16 (over z, y, core).
Axes of the slice: x: 2, y: 2, z: 4, core: 2. Of those that a mesh axis runs over, the one named last changes fastest.
Arguments:
- data_real: bfloat16 [16384, 8192], P(('freq', 'row')), parts along dimension 0, may hold values from -6 to 6
- data_imag: bfloat16 [16384, 8192], P(('freq', 'row')), parts along dimension 0, may hold values from -6 to 6
- counts: int32 [8, 8], replicated, may hold values from 0 to 4
- source_cols: int32 [128], replicated, may hold values from 0 to 8191, as said below
Outputs:
- pred_real: float32 [16384, 128], P(('freq', 'row')), parts along dimension 0
- pred_imag: float32 [16384, 128], P(('freq', 'row')), parts along dimension 0
There are 2 independent parts, one for each index of `freq`. A program takes and returns all parts, laid end to end along the dimension named above; an argument that names none is the same for every part. Nothing has to cross between parts.
Inputs may be any that keep to these rules, and one draw needn't show every extreme that they name: `source_cols`: 128 distinct grid points; 0 and 8191 are always among them.
All inputs are finite; a program needn't handle non-finite values.
Results may differ from a plain program's by a relative error of at most 0.0029.
Values may be sent and summed in bfloat16 or wider, within the bound.
A program may use at most 128 MiB of HBM per device.

v0:
```python
import math
import jax
import jax.numpy as jnp
from jax import lax
from jax.sharding import PartitionSpec as P

TILES = 8


def tile_weights(counts, row_ids, width):
    tile = width // TILES
    onehot = (row_ids[:, None] // tile == jnp.arange(TILES, dtype=jnp.int32)[None, :]).astype(
        jnp.float32
    )
    table = counts.astype(jnp.float32)
    forward = jnp.dot(onehot, table, precision=lax.Precision.HIGHEST)
    backward = jnp.dot(onehot, table.T, precision=lax.Precision.HIGHEST)
    height = row_ids.shape[0]
    forward = jnp.broadcast_to(forward[:, :, None], (height, TILES, tile)).reshape(height, width)
    backward = jnp.broadcast_to(backward[:, :, None], (height, TILES, tile)).reshape(height, width)
    return (forward, backward)


def complex_pair(left_real, left_imag, right_real, right_imag, dims):
    dot_rr = lax.dot_general(left_real, right_real, dims, preferred_element_type=jnp.float32)
    dot_ii = lax.dot_general(left_imag, right_imag, dims, preferred_element_type=jnp.float32)
    dot_ri = lax.dot_general(left_real, right_imag, dims, preferred_element_type=jnp.float32)
    dot_ir = lax.dot_general(left_imag, right_real, dims, preferred_element_type=jnp.float32)
    return jnp.concatenate([dot_rr - dot_ii, dot_ri + dot_ir], axis=1)


def shards(data_real, data_imag, counts, source_cols):
    rows, width = data_real.shape
    mirror_real, mirror_imag = (
        lax.all_to_all(data_real, "row", split_axis=1, concat_axis=0, tiled=True),
        lax.all_to_all(data_imag, "row", split_axis=1, concat_axis=0, tiled=True),
    )
    row_ids = lax.axis_index("row") * rows + jnp.arange(rows, dtype=jnp.int32)
    forward, backward = tile_weights(counts, row_ids, width)
    denom = jnp.maximum(forward + backward, 1.0)
    sym_real = (
        (forward * data_real.astype(jnp.float32) + backward * mirror_real.T.astype(jnp.float32))
        / denom
    ).astype(jnp.bfloat16)
    sym_imag = (
        (forward * data_imag.astype(jnp.float32) + backward * mirror_imag.T.astype(jnp.float32))
        / denom
    ).astype(jnp.bfloat16)
    panel_real = jnp.take(sym_real, source_cols, axis=1)
    panel_imag = jnp.take(sym_imag, source_cols, axis=1)
    sources = source_cols.shape[0]
    factor = -1.0 / math.sqrt(width)
    piece_real = lax.all_gather(panel_real, "row", axis=0, tiled=True)
    piece_imag = lax.all_gather(panel_imag, "row", axis=0, tiled=True)
    summed = complex_pair(sym_real, sym_imag, piece_real, piece_imag, (((1,), (0,)), ((), ())))
    predicted = factor * summed
    return (predicted[:, :sources], predicted[:, sources:])


def solution(mesh):
    placed = (P(("freq", "row"), None), P(("freq", "row"), None), P(), P())
    return jax.shard_map(
        shards,
        mesh=mesh,
        in_specs=placed,
        out_specs=(P(("freq", "row"), None), P(("freq", "row"), None)),
        check_vma=False,
    )
```

profile of v0, /device:TPU:0, one launch (start us, length us, event | category | flops | bytes accessed | tf_op | source)
XLA Modules:
  0.0 530.0 jit_solution(13418963480100498488)
XLA Ops:
  7.2 7.5 %copy.17 = bf16[64,16,8,512]{3,2,0,1:T(8,128)(2,1)} copy(bf16[64,16,8,512]{3,2,1,0:T(8,128)(2,1)} %bitcast.68) | data formatting | bytes 16777216 | tf_op jit(solution)/shard_map/all_to_all | solution.py:35
  14.7 7.4 %all-to-all-start = ((bf16[512,16,512]{2,0,1:T(8,128)(2,1)}), bf16[512,16,512]{2,0,1:T(8,128)(2,1)}, u32[]{:S(2)}, u32[]{:S(2)}) async-start(bf16[512,16,512]{2,0,1:T(8,128)(2,1)} %bitcast.71), calls=%async_computation | async-start | bytes 16777216 | tf_op jit(solution)/shard_map/all_to_all | solution.py:35
  22.1 7.5 %copy.16 = bf16[64,16,8,512]{3,2,0,1:T(8,128)(2,1)} copy(bf16[64,16,8,512]{3,2,1,0:T(8,128)(2,1)} %bitcast.69) | data formatting | bytes 16777216 | tf_op jit(solution)/shard_map/all_to_all | solution.py:36
  29.7 143.2 %all-to-all-done = bf16[512,16,512]{2,0,1:T(8,128)(2,1)} async-done(((bf16[512,16,512]{2,0,1:T(8,128)(2,1)}), bf16[512,16,512]{2,0,1:T(8,128)(2,1)}, u32[]{:S(2)}, u32[]{:S(2)}) %all-to-all-start) | async-done | bytes 8388640 | tf_op jit(solution)/shard_map/all_to_all | solution.py:35
  172.8 36.5 %all-to-all-start.1 = ((bf16[512,16,512]{2,0,1:T(8,128)(2,1)}), bf16[512,16,512]{2,0,1:T(8,128)(2,1)}, u32[]{:S(2)}, u32[]{:S(2)}) async-start(bf16[512,16,512]{2,0,1:T(8,128)(2,1)} %bitcast.70), calls=%async_computation.1 | async-start | bytes 16777216 | tf_op jit(solution)/shard_map/all_to_all | solution.py:36
  209.5 12.0 %copy.6 = bf16[512,8192]{0,1:T(8,128)(2,1)} copy(bf16[512,8192]{1,0:T(8,128)(2,1)} %param.6) | data formatting | bytes 16777216 | tf_op args[0]
  221.5 11.5 %copy.8 = bf16[512,8192]{0,1:T(8,128)(2,1)} copy(bf16[512,8192]{1,0:T(8,128)(2,1)} %param.7) | data formatting | bytes 16777216 | tf_op args[1]
  233.0 0.3 fusion.7
  233.3 0.3 fusion.8
  233.7 126.5 %all-to-all-done.1 = bf16[512,16,512]{2,0,1:T(8,128)(2,1)} async-done(((bf16[512,16,512]{2,0,1:T(8,128)(2,1)}), bf16[512,16,512]{2,0,1:T(8,128)(2,1)}, u32[]{:S(2)}, u32[]{:S(2)}) %all-to-all-start.1) | async-done | bytes 8388640 | tf_op jit(solution)/shard_map/all_to_all | solution.py:36
  360.1 18.6 %fusion.2 = (bf16[512,8192]{0,1:T(8,128)(2,1)}, bf16[512,8192]{0,1:T(8,128)(2,1)}) fusion(bf16[512,8192]{0,1:T(8,128)(2,1)} %copy.6, f32[512,8]{0,1:T(8,128)S(1)} %fusion.7, f32[512,8]{0,1:T(8,128)S(1)} %fusion.8, bf16[512,16,512]{2,0,1:T(8,128)(2,1)} %all-to-all-done, bf16[512,16,512]{2,0,1:T(8,128)(2,1)} %all-to-all-done.1, bf16[512,8192]{0,1:T(8,128)(2,1)} %copy.8), kind=kLoop, calls=%fused_computation.9 | loop fusion | flops 67108864 | bytes 50364416 | tf_op jit(solution)/shard_map/convert_element_type | solution.py:44
  378.7 5.3 %gather_fusion = bf16[128,512]{1,0:T(8,128)(2,1)S(1)} fusion(bf16[512,8192]{0,1:T(8,128)(2,1)} %get-tuple-element.7, s32[1024]{0:T(1024)S(1)} %pad_clamp_fusion), kind=kCustom, calls=%fused_computation.clone | custom fusion | bytes 262656 | tf_op jit(solution)/shard_map/jit(_take)/gather | solution.py:49
  384.0 5.3 %gather_fusion.1 = bf16[128,512]{1,0:T(8,128)(2,1)S(1)} fusion(bf16[512,8192]{0,1:T(8,128)(2,1)} %get-tuple-element.8, s32[1024]{0:T(1024)S(1)} %pad_clamp_fusion), kind=kCustom, calls=%fused_computation.1.clone | custom fusion | bytes 262656 | tf_op jit(solution)/shard_map/jit(_take)/gather | solution.py:50
  389.3 0.8 select_bitcast_fusion.1
  390.2 0.2 all-gather.5.cloned.1.call-start
  390.4 0.5 all-gather.5.cloned.1.call-update
  390.9 72.4 %all-gather.3.cloned.1.call-done = bf16[8192,128]{0,1:T(8,128)(2,1)} async-done(((bf16[512,128]{0,1:T(8,128)(2,1)}), bf16[8192,128]{0,1:T(8,128)(2,1)}) %all-gather.3.cloned.1.call-update) | async-done | bytes 2097168 | tf_op jit(solution)/shard_map/all_gather | solution.py:53
  463.3 5.3 fusion.17
  468.6 37.6 %all-gather.5.cloned.1.call-done = bf16[8192,128]{0,1:T(8,128)(2,1)} async-done(((bf16[512,128]{0,1:T(8,128)(2,1)}), bf16[8192,128]{0,1:T(8,128)(2,1)}) %all-gather.5.cloned.1.call-update) | async-done | bytes 2097168 | tf_op jit(solution)/shard_map/all_gather | solution.py:54
  506.2 5.4 %fusion.18 = f32[512,128]{0,1:T(8,128)S(1)} fusion(bf16[8192,128]{0,1:T(8,128)(2,1)} %all-gather.5.cloned.1.call-done, bf16[512,8192]{0,1:T(8,128)(2,1)} %get-tuple-element.7), kind=kOutput, calls=%fused_computation.42 | convolution fusion | flops 1073741824 | bytes 10747904 | tf_op jit(solution)/shard_map/dot_general | solution.py:27
  511.6 4.9 convolution_subtract_fusion
  516.6 4.8 convolution_add_fusion
  521.5 0.8 copy.10
  522.3 0.8 copy.11
  (16 shorter events, 0.2 us)
Async XLA Ops:
  14.7 158.2 %all-to-all-start = ((bf16[512,16,512]{2,0,1:T(8,128)(2,1)}), bf16[512,16,512]{2,0,1:T(8,128)(2,1)}, u32[]{:S(2)}, u32[]{:S(2)}) async-start(bf16[512,16,512]{2,0,1:T(8,128)(2,1)} %bitcast.71), calls=%async_computation | async-start | bytes 16777216 | tf_op jit(solution)/shard_map/all_to_all | solution.py:35
  172.8 187.3 %all-to-all-start.1 = ((bf16[512,16,512]{2,0,1:T(8,128)(2,1)}), bf16[512,16,512]{2,0,1:T(8,128)(2,1)}, u32[]{:S(2)}, u32[]{:S(2)}) async-start(bf16[512,16,512]{2,0,1:T(8,128)(2,1)} %bitcast.70), calls=%async_computation.1 | async-start | bytes 16777216 | tf_op jit(solution)/shard_map/all_to_all | solution.py:36
  209.4 253.9 %all-gather.3.cloned.1.call-start = ((), (), s32[]{:S(2)}) async-start(), calls=%async_computation.2 | async-start | bytes 2228224 | tf_op jit(solution)/shard_map/all_gather | solution.py:53
  221.4 11.5 %copy-start.3 = (s32[128]{0:T(128)S(1)}, s32[128]{0:T(128)}, u32[]{:S(2)}) copy-start(s32[128]{0:T(128)} %param.9) | copy-start | bytes 1540
  221.5 11.6 %copy-start.2 = (s32[8,8]{1,0:T(8,128)S(1)}, s32[8,8]{1,0:T(8,128)}, u32[]{:S(2)}) copy-start(s32[8,8]{1,0:T(8,128)} %param.8) | copy-start | bytes 772
  390.2 116.0 %all-gather.5.cloned.1.call-start = ((), (), s32[]{:S(2)}) async-start(), calls=%async_computation.3 | async-start | bytes 2228224 | tf_op jit(solution)/shard_map/all_gather | solution.py:54
  506.2 5.4 %copy-start.1 = (bf16[8192,128]{0,1:T(8,128)(2,1)S(1)}, bf16[8192,128]{0,1:T(8,128)(2,1)}, u32[]{:S(2)}) copy-start(bf16[8192,128]{0,1:T(8,128)(2,1)} %all-gather.5.cloned.1.call-done) | copy-start | bytes 6291460
  511.6 4.9 copy-start
Sparse Core Ops, SparseCore 0:
  390.3 72.9 all-gather.2
  466.0 40.1 all-gather.4
where the time goes:
time: 531 us; the launch traced here: 530 us
  waiting for transfers between devices  380 us (72%)
  local copies, waits for them, and re-layouts  50.9 us (10%)
  starting transfers between devices  44.2 us (8%)
  matrix products  21 us (4%)
  other arithmetic  19.4 us (4%)
  between operations  14.2 us (3%)
    all_to_all x1, waiting for transfers between devices, shards(): lax.all_to_all(data_real, 'row', split_axis=1, concat_axis=0, tiled=True)  143 us
    all_to_all x1, waiting for transfers between devices, shards(): lax.all_to_all(data_imag, 'row', split_axis=1, concat_axis=0, tiled=True)  126 us
    all_gather x1, waiting for transfers between devices, shards(): piece_real = lax.all_gather(panel_real, 'row', axis=0, tiled=True)  72.4 us
    all_gather x1, waiting for transfers between devices, shards(): piece_imag = lax.all_gather(panel_imag, 'row', axis=0, tiled=True)  37.6 us
    all_to_all x1, starting transfers between devices, shards(): lax.all_to_all(data_imag, 'row', split_axis=1, concat_axis=0, tiled=True)  36.5 us
    unnamed x12, local copies, waits for them, and re-layouts  25.2 us
    convert_element_type x1, other arithmetic, shards(): sym_real = ((forward * data_real.astype(jnp.float32) + backward * mirror_...  18.6 us
  transfers between devices with their start and end apart: 4, of which 4 were waited for; matrix products, arithmetic and copies ran while one was open for 7% of the time, Pallas kernels for 0%

commit v1 on v0

--- a/solution.py
+++ b/solution.py
@@ -51,7 +51,12 @@
     sources = source_cols.shape[0]
     factor = -1.0 / math.sqrt(width)
     piece_real = lax.all_gather(panel_real, "row", axis=0, tiled=True)
-    piece_imag = lax.all_gather(panel_imag, "row", axis=0, tiled=True)
+    ring = [panel_imag]
+    for hop in range(15):
+        ring.append(lax.ppermute(ring[-1], "row", [(dev, (dev + 1) % 16) for dev in range(16)]))
+    piece_imag = jnp.roll(
+        jnp.concatenate(ring[::-1], axis=0), (lax.axis_index("row") + 1) * ring[0].shape[0], axis=0
+    )
     summed = complex_pair(sym_real, sym_imag, piece_real, piece_imag, (((1,), (0,)), ((), ())))
     predicted = factor * summed
     return (predicted[:, :sources], predicted[:, sources:])

time: 531 us -> 585 us (1.10)
  waiting for transfers between devices: 380 us -> 413 us
  local copies, waits for them, and re-layouts: 50.9 us -> 73.1 us
    ppermute x0 -> x15, waiting for transfers between devices: none -> 136 us  [shards(): lax.ppermute(ring[-1], 'row', [(dev, (dev + 1) % 16) for dev in range(16)])]
    all_gather x1, waiting for transfers between devices: 72.4 us -> 7.65 us  [shards(): piece_real = lax.all_gather(panel_real, 'row', axis=0, tiled=True)]
    all_gather x1 -> x0, waiting for transfers between devices: 37.6 us -> none  [shards(): piece_imag = lax.all_gather(panel_imag, 'row', axis=0, tiled=True)]
    unnamed x12 -> x45, local copies, waits for them, and re-layouts: 25.2 us -> 46.6 us
  transfers between devices with their start and end apart: 4 -> 18, of which waited for: 4 -> 18; matrix products, arithmetic and copies ran while one was open for 7% -> 9% of each run, Pallas kernels for 0% -> 0%
where the time goes in v1:
time: 585 us; the launch traced here: 584 us
  waiting for transfers between devices  413 us (71%)
  local copies, waits for them, and re-layouts  73.1 us (12%)
  starting transfers between devices  44.8 us (8%)
  other arithmetic  19.4 us (3%)
  matrix products  19.2 us (3%)
  between operations  14.2 us (2%)
    all_to_all x1, waiting for transfers between devices, shards(): lax.all_to_all(data_real, 'row', split_axis=1, concat_axis=0, tiled=True)  143 us
    ppermute x15, waiting for transfers between devices, shards(): lax.ppermute(ring[-1], 'row', [(dev, (dev + 1) % 16) for dev in range(16)])  136 us
    all_to_all x1, waiting for transfers between devices, shards(): lax.all_to_all(data_imag, 'row', split_axis=1, concat_axis=0, tiled=True)  126 us
    unnamed x45, local copies, waits for them, and re-layouts  46.6 us
    all_to_all x1, starting transfers between devices, shards(): lax.all_to_all(data_imag, 'row', split_axis=1, concat_axis=0, tiled=True)  36.5 us
    convert_element_type x1, other arithmetic, shards(): sym_imag = ((forward * data_imag.astype(jnp.float32) + backward * mirror_...  18.6 us
  transfers between devices with their start and end apart: 18, of which 18 were waited for; matrix products, arithmetic and copies ran while one was open for 9% of the time, Pallas kernels for 0%

profile of v1, /device:TPU:0, one launch (start us, length us, event | category | flops | bytes accessed | tf_op | source)
XLA Modules:
  0.0 583.9 jit_solution(3168229009392243795)
XLA Ops:
  7.2 7.5 %copy.17 = bf16[64,16,8,512]{3,2,0,1:T(8,128)(2,1)} copy(bf16[64,16,8,512]{3,2,1,0:T(8,128)(2,1)} %bitcast.68) | data formatting | bytes 16777216 | tf_op jit(solution)/shard_map/all_to_all | solution.py:35
  14.7 7.4 %all-to-all-start = ((bf16[512,16,512]{2,0,1:T(8,128)(2,1)}), bf16[512,16,512]{2,0,1:T(8,128)(2,1)}, u32[]{:S(2)}, u32[]{:S(2)}) async-start(bf16[512,16,512]{2,0,1:T(8,128)(2,1)} %bitcast.71), calls=%async_computation | async-start | bytes 16777216 | tf_op jit(solution)/shard_map/all_to_all | solution.py:35
  22.1 7.6 %copy.16 = bf16[64,16,8,512]{3,2,0,1:T(8,128)(2,1)} copy(bf16[64,16,8,512]{3,2,1,0:T(8,128)(2,1)} %bitcast.69) | data formatting | bytes 16777216 | tf_op jit(solution)/shard_map/all_to_all | solution.py:36
  29.7 143.1 %all-to-all-done = bf16[512,16,512]{2,0,1:T(8,128)(2,1)} async-done(((bf16[512,16,512]{2,0,1:T(8,128)(2,1)}), bf16[512,16,512]{2,0,1:T(8,128)(2,1)}, u32[]{:S(2)}, u32[]{:S(2)}) %all-to-all-start) | async-done | bytes 8388640 | tf_op jit(solution)/shard_map/all_to_all | solution.py:35
  172.8 36.5 %all-to-all-start.1 = ((bf16[512,16,512]{2,0,1:T(8,128)(2,1)}), bf16[512,16,512]{2,0,1:T(8,128)(2,1)}, u32[]{:S(2)}, u32[]{:S(2)}) async-start(bf16[512,16,512]{2,0,1:T(8,128)(2,1)} %bitcast.70), calls=%async_computation.1 | async-start | bytes 16777216 | tf_op jit(solution)/shard_map/all_to_all | solution.py:36
  209.4 11.8 %copy.6 = bf16[512,8192]{0,1:T(8,128)(2,1)} copy(bf16[512,8192]{1,0:T(8,128)(2,1)} %param.6) | data formatting | bytes 16777216 | tf_op args[0]
  221.3 12.0 %copy.8 = bf16[512,8192]{0,1:T(8,128)(2,1)} copy(bf16[512,8192]{1,0:T(8,128)(2,1)} %param.7) | data formatting | bytes 16777216 | tf_op args[1]
  234.0 126.1 %all-to-all-done.1 = bf16[512,16,512]{2,0,1:T(8,128)(2,1)} async-done(((bf16[512,16,512]{2,0,1:T(8,128)(2,1)}), bf16[512,16,512]{2,0,1:T(8,128)(2,1)}, u32[]{:S(2)}, u32[]{:S(2)}) %all-to-all-start.1) | async-done | bytes 8388640 | tf_op jit(solution)/shard_map/all_to_all | solution.py:36
  360.1 18.6 %fusion.5 = (bf16[512,8192]{0,1:T(8,128)(2,1)}, bf16[512,8192]{0,1:T(8,128)(2,1)}) fusion(bf16[512,8192]{0,1:T(8,128)(2,1)} %copy.8, f32[512,8]{0,1:T(8,128)S(1)} %fusion.17, f32[512,8]{0,1:T(8,128)S(1)} %fusion.18, bf16[512,16,512]{2,0,1:T(8,128)(2,1)} %all-to-all-done.1, bf16[512,16,512]{2,0,1:T(8,128)(2,1)} %all-to-all-done, bf16[512,8192]{0,1:T(8,128)(2,1)} %copy.6), kind=kLoop, calls=%fused_computation.12 | loop fusion | flops 67108864 | bytes 50364416 | tf_op jit(solution)/shard_map/convert_element_type | solution.py:48
  390.8 36.9 %collective-permute-done = bf16[512,128]{0,1:T(8,128)(2,1)S(1)} collective-permute-done((bf16[512,128]{0,1:T(8,128)(2,1)S(1)}, bf16[512,128]{0,1:T(8,128)(2,1)S(1)}, u32[]{:S(2)}, u32[]{:S(2)}) %collective-permute-start) | collective-permute-done | bytes 131104 | tf_op jit(solution)/shard_map/ppermute | solution.py:56
  427.7 7.1 %collective-permute-done.1 = bf16[512,128]{0,1:T(8,128)(2,1)S(1)} collective-permute-done((bf16[512,128]{0,1:T(8,128)(2,1)S(1)}, bf16[512,128]{0,1:T(8,128)(2,1)S(1)}, u32[]{:S(2)}, u32[]{:S(2)}) %collective-permute-start.1) | collective-permute-done | bytes 131104 | tf_op jit(solution)/shard_map/ppermute | solution.py:56
  434.8 7.1 %collective-permute-done.2 = bf16[512,128]{0,1:T(8,128)(2,1)S(1)} collective-permute-done((bf16[512,128]{0,1:T(8,128)(2,1)S(1)}, bf16[512,128]{0,1:T(8,128)(2,1)S(1)}, u32[]{:S(2)}, u32[]{:S(2)}) %collective-permute-start.2) | collective-permute-done | bytes 131104 | tf_op jit(solution)/shard_map/ppermute | solution.py:56
  441.9 7.1 %collective-permute-done.3 = bf16[512,128]{0,1:T(8,128)(2,1)S(1)} collective-permute-done((bf16[512,128]{0,1:T(8,128)(2,1)S(1)}, bf16[512,128]{0,1:T(8,128)(2,1)S(1)}, u32[]{:S(2)}, u32[]{:S(2)}) %collective-permute-start.3) | collective-permute-done | bytes 131104 | tf_op jit(solution)/shard_map/ppermute | solution.py:56
  449.0 7.1 %collective-permute-done.4 = bf16[512,128]{0,1:T(8,128)(2,1)S(1)} collective-permute-done((bf16[512,128]{0,1:T(8,128)(2,1)S(1)}, bf16[512,128]{0,1:T(8,128)(2,1)S(1)}, u32[]{:S(2)}, u32[]{:S(2)}) %collective-permute-start.4) | collective-permute-done | bytes 131104 | tf_op jit(solution)/shard_map/ppermute | solution.py:56
  456.1 7.1 %collective-permute-done.5 = bf16[512,128]{0,1:T(8,128)(2,1)S(1)} collective-permute-done((bf16[512,128]{0,1:T(8,128)(2,1)S(1)}, bf16[512,128]{0,1:T(8,128)(2,1)S(1)}, u32[]{:S(2)}, u32[]{:S(2)}) %collective-permute-start.5) | collective-permute-done | bytes 131104 | tf_op jit(solution)/shard_map/ppermute | solution.py:56
  463.2 7.1 %collective-permute-done.6 = bf16[512,128]{0,1:T(8,128)(2,1)S(1)} collective-permute-done((bf16[512,128]{0,1:T(8,128)(2,1)S(1)}, bf16[512,128]{0,1:T(8,128)(2,1)S(1)}, u32[]{:S(2)}, u32[]{:S(2)}) %collective-permute-start.6) | collective-permute-done | bytes 131104 | tf_op jit(solution)/shard_map/ppermute | solution.py:56
  470.3 7.1 %collective-permute-done.7 = bf16[512,128]{0,1:T(8,128)(2,1)S(1)} collective-permute-done((bf16[512,128]{0,1:T(8,128)(2,1)S(1)}, bf16[512,128]{0,1:T(8,128)(2,1)S(1)}, u32[]{:S(2)}, u32[]{:S(2)}) %collective-permute-start.7) | collective-permute-done | bytes 131104 | tf_op jit(solution)/shard_map/ppermute | solution.py:56
  477.4 7.1 %collective-permute-done.8 = bf16[512,128]{0,1:T(8,128)(2,1)S(1)} collective-permute-done((bf16[512,128]{0,1:T(8,128)(2,1)S(1)}, bf16[512,128]{0,1:T(8,128)(2,1)S(1)}, u32[]{:S(2)}, u32[]{:S(2)}) %collective-permute-start.8) | collective-permute-done | bytes 131104 | tf_op jit(solution)/shard_map/ppermute | solution.py:56
  484.5 7.1 %collective-permute-done.9 = bf16[512,128]{0,1:T(8,128)(2,1)S(1)} collective-permute-done((bf16[512,128]{0,1:T(8,128)(2,1)S(1)}, bf16[512,128]{0,1:T(8,128)(2,1)S(1)}, u32[]{:S(2)}, u32[]{:S(2)}) %collective-permute-start.9) | collective-permute-done | bytes 131104 | tf_op jit(solution)/shard_map/ppermute | solution.py:56
  491.6 7.1 %collective-permute-done.10 = bf16[512,128]{0,1:T(8,128)(2,1)S(1)} collective-permute-done((bf16[512,128]{0,1:T(8,128)(2,1)S(1)}, bf16[512,128]{0,1:T(8,128)(2,1)S(1)}, u32[]{:S(2)}, u32[]{:S(2)}) %collective-permute-start.10) | collective-permute-done | bytes 131104 | tf_op jit(solution)/shard_map/ppermute | solution.py:56
  498.6 7.1 %collective-permute-done.11 = bf16[512,128]{0,1:T(8,128)(2,1)S(1)} collective-permute-done((bf16[512,128]{0,1:T(8,128)(2,1)S(1)}, bf16[512,128]{0,1:T(8,128)(2,1)S(1)}, u32[]{:S(2)}, u32[]{:S(2)}) %collective-permute-start.11) | collective-permute-done | bytes 131104 | tf_op jit(solution)/shard_map/ppermute | solution.py:56
  505.7 7.1 %collective-permute-done.12 = bf16[512,128]{0,1:T(8,128)(2,1)S(1)} collective-permute-done((bf16[512,128]{0,1:T(8,128)(2,1)S(1)}, bf16[512,128]{0,1:T(8,128)(2,1)S(1)}, u32[]{:S(2)}, u32[]{:S(2)}) %collective-permute-start.12) | collective-permute-done | bytes 131104 | tf_op jit(solution)/shard_map/ppermute | solution.py:56
  519.9 7.3 %collective-permute-done.14 = bf16[512,128]{0,1:T(8,128)(2,1)S(1)} collective-permute-done((bf16[512,128]{0,1:T(8,128)(2,1)S(1)}, bf16[512,128]{0,1:T(8,128)(2,1)S(1)}, u32[]{:S(2)}, u32[]{:S(2)}) %collective-permute-start.14) | collective-permute-done | bytes 131104 | tf_op jit(solution)/shard_map/ppermute | solution.py:56
  548.9 7.6 %all-gather.2.cloned.1.call-done = bf16[8192,128]{0,1:T(8,128)(2,1)} async-done(((bf16[512,128]{0,1:T(8,128)(2,1)}), bf16[8192,128]{0,1:T(8,128)(2,1)}) %all-gather.2.cloned.1.call-update) | async-done | bytes 2097168 | tf_op jit(solution)/shard_map/all_gather | solution.py:53
  (78 shorter events, 62.1 us)
Async XLA Ops:
  14.7 158.2 %all-to-all-start = ((bf16[512,16,512]{2,0,1:T(8,128)(2,1)}), bf16[512,16,512]{2,0,1:T(8,128)(2,1)}, u32[]{:S(2)}, u32[]{:S(2)}) async-start(bf16[512,16,512]{2,0,1:T(8,128)(2,1)} %bitcast.71), calls=%async_computation | async-start | bytes 16777216 | tf_op jit(solution)/shard_map/all_to_all | solution.py:35
  172.8 187.3 %all-to-all-start.1 = ((bf16[512,16,512]{2,0,1:T(8,128)(2,1)}), bf16[512,16,512]{2,0,1:T(8,128)(2,1)}, u32[]{:S(2)}, u32[]{:S(2)}) async-start(bf16[512,16,512]{2,0,1:T(8,128)(2,1)} %bitcast.70), calls=%async_computation.1 | async-start | bytes 16777216 | tf_op jit(solution)/shard_map/all_to_all | solution.py:36
  209.4 347.2 %all-gather.2.cloned.1.call-start = ((), (), s32[]{:S(2)}) async-start(), calls=%async_computation.2 | async-start | bytes 2228224 | tf_op jit(solution)/shard_map/all_gather | solution.py:53
  221.3 12.0 %copy-start.2 = (s32[128]{0:T(128)S(1)}, s32[128]{0:T(128)}, u32[]{:S(2)}) copy-start(s32[128]{0:T(128)} %param.9) | copy-start | bytes 1540
  221.3 12.1 %copy-start.1 = (s32[8,8]{1,0:T(8,128)S(1)}, s32[8,8]{1,0:T(8,128)}, u32[]{:S(2)}) copy-start(s32[8,8]{1,0:T(8,128)} %param.8) | copy-start | bytes 772
  390.1 37.7 %collective-permute-start = (bf16[512,128]{0,1:T(8,128)(2,1)S(1)}, bf16[512,128]{0,1:T(8,128)(2,1)S(1)}, u32[]{:S(2)}, u32[]{:S(2)}) collective-permute-start(bf16[512,128]{0,1:T(8,128)(2,1)S(1)} %get-tuple-element.9), channel_id=1, source_target_pairs={{0,1},{1,2},{2,3},{3,4},{4,5},{5,6},{6,7},{7,8},{8,9},{9,10},{10,1... | collective-permute-start | bytes 393224 | tf_op jit(solution)/shard_map/ppermute | solution.py:56
  427.7 7.1 %collective-permute-start.1 = (bf16[512,128]{0,1:T(8,128)(2,1)S(1)}, bf16[512,128]{0,1:T(8,128)(2,1)S(1)}, u32[]{:S(2)}, u32[]{:S(2)}) collective-permute-start(bf16[512,128]{0,1:T(8,128)(2,1)S(1)} %collective-permute-done), channel_id=1, source_target_pairs={{0,1},{1,2},{2,3},{3,4},{4,5},{5,6},{6,7},{7,8},{8,9},{9,10},{10,1... | collective-permute-start | bytes 393224 | tf_op jit(solution)/shard_map/ppermute | solution.py:56
  434.8 7.1 %collective-permute-start.2 = (bf16[512,128]{0,1:T(8,128)(2,1)S(1)}, bf16[512,128]{0,1:T(8,128)(2,1)S(1)}, u32[]{:S(2)}, u32[]{:S(2)}) collective-permute-start(bf16[512,128]{0,1:T(8,128)(2,1)S(1)} %collective-permute-done.1), channel_id=1, source_target_pairs={{0,1},{1,2},{2,3},{3,4},{4,5},{5,6},{6,7},{7,8},{8,9},{9,10},{10,1... | collective-permute-start | bytes 393224 | tf_op jit(solution)/shard_map/ppermute | solution.py:56
  441.9 7.1 %collective-permute-start.3 = (bf16[512,128]{0,1:T(8,128)(2,1)S(1)}, bf16[512,128]{0,1:T(8,128)(2,1)S(1)}, u32[]{:S(2)}, u32[]{:S(2)}) collective-permute-start(bf16[512,128]{0,1:T(8,128)(2,1)S(1)} %collective-permute-done.2), channel_id=1, source_target_pairs={{0,1},{1,2},{2,3},{3,4},{4,5},{5,6},{6,7},{7,8},{8,9},{9,10},{10,1... | collective-permute-start | bytes 393224 | tf_op jit(solution)/shard_map/ppermute | solution.py:56
  449.0 7.1 %collective-permute-start.4 = (bf16[512,128]{0,1:T(8,128)(2,1)S(1)}, bf16[512,128]{0,1:T(8,128)(2,1)S(1)}, u32[]{:S(2)}, u32[]{:S(2)}) collective-permute-start(bf16[512,128]{0,1:T(8,128)(2,1)S(1)} %collective-permute-done.3), channel_id=1, source_target_pairs={{0,1},{1,2},{2,3},{3,4},{4,5},{5,6},{6,7},{7,8},{8,9},{9,10},{10,1... | collective-permute-start | bytes 393224 | tf_op jit(solution)/shard_map/ppermute | solution.py:56
  456.1 7.1 %collective-permute-start.5 = (bf16[512,128]{0,1:T(8,128)(2,1)S(1)}, bf16[512,128]{0,1:T(8,128)(2,1)S(1)}, u32[]{:S(2)}, u32[]{:S(2)}) collective-permute-start(bf16[512,128]{0,1:T(8,128)(2,1)S(1)} %collective-permute-done.4), channel_id=1, source_target_pairs={{0,1},{1,2},{2,3},{3,4},{4,5},{5,6},{6,7},{7,8},{8,9},{9,10},{10,1... | collective-permute-start | bytes 393224 | tf_op jit(solution)/shard_map/ppermute | solution.py:56
  463.2 7.1 %collective-permute-start.6 = (bf16[512,128]{0,1:T(8,128)(2,1)S(1)}, bf16[512,128]{0,1:T(8,128)(2,1)S(1)}, u32[]{:S(2)}, u32[]{:S(2)}) collective-permute-start(bf16[512,128]{0,1:T(8,128)(2,1)S(1)} %collective-permute-done.5), channel_id=1, source_target_pairs={{0,1},{1,2},{2,3},{3,4},{4,5},{5,6},{6,7},{7,8},{8,9},{9,10},{10,1... | collective-permute-start | bytes 393224 | tf_op jit(solution)/shard_map/ppermute | solution.py:56
  470.3 7.1 %collective-permute-start.7 = (bf16[512,128]{0,1:T(8,128)(2,1)S(1)}, bf16[512,128]{0,1:T(8,128)(2,1)S(1)}, u32[]{:S(2)}, u32[]{:S(2)}) collective-permute-start(bf16[512,128]{0,1:T(8,128)(2,1)S(1)} %collective-permute-done.6), channel_id=1, source_target_pairs={{0,1},{1,2},{2,3},{3,4},{4,5},{5,6},{6,7},{7,8},{8,9},{9,10},{10,1... | collective-permute-start | bytes 393224 | tf_op jit(solution)/shard_map/ppermute | solution.py:56
  477.4 7.1 %collective-permute-start.8 = (bf16[512,128]{0,1:T(8,128)(2,1)S(1)}, bf16[512,128]{0,1:T(8,128)(2,1)S(1)}, u32[]{:S(2)}, u32[]{:S(2)}) collective-permute-start(bf16[512,128]{0,1:T(8,128)(2,1)S(1)} %collective-permute-done.7), channel_id=1, source_target_pairs={{0,1},{1,2},{2,3},{3,4},{4,5},{5,6},{6,7},{7,8},{8,9},{9,10},{10,1... | collective-permute-start | bytes 393224 | tf_op jit(solution)/shard_map/ppermute | solution.py:56
  484.5 7.1 %collective-permute-start.9 = (bf16[512,128]{0,1:T(8,128)(2,1)S(1)}, bf16[512,128]{0,1:T(8,128)(2,1)S(1)}, u32[]{:S(2)}, u32[]{:S(2)}) collective-permute-start(bf16[512,128]{0,1:T(8,128)(2,1)S(1)} %collective-permute-done.8), channel_id=1, source_target_pairs={{0,1},{1,2},{2,3},{3,4},{4,5},{5,6},{6,7},{7,8},{8,9},{9,10},{10,1... | collective-permute-start | bytes 393224 | tf_op jit(solution)/shard_map/ppermute | solution.py:56
  491.6 7.1 %collective-permute-start.10 = (bf16[512,128]{0,1:T(8,128)(2,1)S(1)}, bf16[512,128]{0,1:T(8,128)(2,1)S(1)}, u32[]{:S(2)}, u32[]{:S(2)}) collective-permute-start(bf16[512,128]{0,1:T(8,128)(2,1)S(1)} %collective-permute-done.9), channel_id=1, source_target_pairs={{0,1},{1,2},{2,3},{3,4},{4,5},{5,6},{6,7},{7,8},{8,9},{9,10},{10,1... | collective-permute-start | bytes 393224 | tf_op jit(solution)/shard_map/ppermute | solution.py:56
  498.6 7.1 %collective-permute-start.11 = (bf16[512,128]{0,1:T(8,128)(2,1)S(1)}, bf16[512,128]{0,1:T(8,128)(2,1)S(1)}, u32[]{:S(2)}, u32[]{:S(2)}) collective-permute-start(bf16[512,128]{0,1:T(8,128)(2,1)S(1)} %collective-permute-done.10), channel_id=1, source_target_pairs={{0,1},{1,2},{2,3},{3,4},{4,5},{5,6},{6,7},{7,8},{8,9},{9,10},{10,1... | collective-permute-start | bytes 393224 | tf_op jit(solution)/shard_map/ppermute | solution.py:56
  505.7 7.1 %collective-permute-start.12 = (bf16[512,128]{0,1:T(8,128)(2,1)S(1)}, bf16[512,128]{0,1:T(8,128)(2,1)S(1)}, u32[]{:S(2)}, u32[]{:S(2)}) collective-permute-start(bf16[512,128]{0,1:T(8,128)(2,1)S(1)} %collective-permute-done.11), channel_id=1, source_target_pairs={{0,1},{1,2},{2,3},{3,4},{4,5},{5,6},{6,7},{7,8},{8,9},{9,10},{10,1... | collective-permute-start | bytes 393224 | tf_op jit(solution)/shard_map/ppermute | solution.py:56
  512.8 7.1 %collective-permute-start.13 = (bf16[512,128]{0,1:T(8,128)(2,1)S(1)}, bf16[512,128]{0,1:T(8,128)(2,1)S(1)}, u32[]{:S(2)}, u32[]{:S(2)}) collective-permute-start(bf16[512,128]{0,1:T(8,128)(2,1)S(1)} %collective-permute-done.12), channel_id=1, source_target_pairs={{0,1},{1,2},{2,3},{3,4},{4,5},{5,6},{6,7},{7,8},{8,9},{9,10},{10,1... | collective-permute-start | bytes 393224 | tf_op jit(solution)/shard_map/ppermute | solution.py:56
  519.9 7.3 %collective-permute-start.14 = (bf16[512,128]{0,1:T(8,128)(2,1)S(1)}, bf16[512,128]{0,1:T(8,128)(2,1)S(1)}, u32[]{:S(2)}, u32[]{:S(2)}) collective-permute-start(bf16[512,128]{0,1:T(8,128)(2,1)S(1)} %collective-permute-done.13), channel_id=1, source_target_pairs={{0,1},{1,2},{2,3},{3,4},{4,5},{5,6},{6,7},{7,8},{8,9},{9,10},{10,1... | collective-permute-start | bytes 393224 | tf_op jit(solution)/shard_map/ppermute | solution.py:56
  561.9 5.5 copy-start
  561.9 10.4 %slice-start = ((s8[8388608]{0:T(1024)(128)(4,1)}), s8[4194304]{0:T(1024)(128)(4,1)S(1)}, s32[]{:S(2)}) async-start(s8[8388608]{0:T(1024)(128)(4,1)} %bitcast.66), calls=%async_computation.3 | async-start | bytes 8388608
  567.3 4.9 slice-start.1
Sparse Core Ops, SparseCore 0:
  513.0 43.5 all-gather.1
